TPU v7x, 256 devices: a whole 4x4x8 slice. The times are simulated.
256 devices in a mesh: tm: 128 (over y, x, z), tok: 2 (over core).
Axes of the slice: x: 4, y: 4, z: 8, core: 2. Of those that a mesh axis runs over, the one named last changes fastest.
Arguments:
- patches: bfloat16 [128, 12, 12, 12, 512], P('tm', 'tok'), may hold values from -6 to 6
- patch_weight: bfloat16 [512, 512], replicated, may hold values from -0.25 to 0.25
- conv_taps: bfloat16 [27, 512], replicated, may hold values from -2 to 2
- gain_space: bfloat16 [512], replicated, may hold values from 0.099609375 to 1.8984375
- qkv_space: bfloat16 [512, 1536], replicated, may hold values from -0.25 to 0.25
- out_space: bfloat16 [512, 512], replicated, may hold values from -0.25 to 0.25
- gain_time: bfloat16 [512], replicated, may hold values from 0.099609375 to 1.8984375
- qkv_time: bfloat16 [512, 1536], replicated, may hold values from -0.25 to 0.25
- out_time: bfloat16 [512, 512], replicated, may hold values from -0.25 to 0.25
Outputs:
- block_out: bfloat16 [128, 12, 12, 12, 512], P('tm', 'tok')
All inputs are finite; a program needn't handle non-finite values.
Results may differ from a plain program's by a relative error of at most 0.018.
Values may be sent and summed in bfloat16 or wider, within the bound.
A program may use at most 128 MiB of HBM per device.

v0:
```python
import jax
import jax.numpy as jnp
from jax import lax
from jax.sharding import PartitionSpec as P
from jax.experimental import pallas as pl
from jax.experimental.pallas import tpu as pltpu
import functools

D = 512
H = 8
WIN = 4


def extended(block, sides, width):
    for axis, dim in sides:
        count = lax.axis_size(axis)
        forward = [(i, i + 1) for i in range(count - 1)]
        backward = [(target, source) for source, target in forward]
        low = lax.ppermute(
            lax.slice_in_dim(block, block.shape[dim] - width, None, axis=dim), axis, forward
        )
        high = lax.ppermute(lax.slice_in_dim(block, 0, width, axis=dim), axis, backward)
        block = jnp.concatenate([low, block, high], axis=dim)
    return block


def from_behind(value, axis, steps):
    count = lax.axis_size(axis)
    leading, last = (max(0, -steps), min(count, count - steps))
    return lax.ppermute(value, axis, [(source, source + steps) for source in range(leading, last)])


def rms_scale(values, gain):
    mean_sq = jnp.mean(values * values, axis=-1, keepdims=True)
    return values * lax.rsqrt(mean_sq + 1e-06) * gain.astype(jnp.float32)


def split_heads(block, count, head_size):
    return block.reshape(block.shape[0], count, head_size).transpose(1, 0, 2)


def attend(query, keys, values):
    rows, cols = query.shape
    head_size = D // H
    count = cols // head_size
    scale = head_size ** (-0.5)

    def one_head(parts):
        q_one, k_one, v_one = parts
        scores = jnp.dot(q_one, k_one.T, preferred_element_type=jnp.float32) * scale
        expo = jnp.exp(scores)
        mixed = jnp.dot(expo.astype(jnp.bfloat16), v_one, preferred_element_type=jnp.float32)
        return (mixed / jnp.sum(expo, axis=-1, keepdims=True)).astype(jnp.bfloat16)

    parts = (
        split_heads(query, count, head_size),
        split_heads(keys, count, head_size),
        split_heads(values, count, head_size),
    )
    result = lax.map(one_head, parts)
    return result.transpose(1, 0, 2).reshape(rows, cols)


def pair_attention_kernel(q_ref, k_ref, v_ref, o_ref):
    head_size = D // H
    scale = head_size ** (-0.5)
    q = q_ref[...]
    k = k_ref[...]
    v = v_ref[...]
    lane = lax.broadcasted_iota(jnp.int32, (1, q.shape[1]), 1)
    first = lane < head_size
    outs = []
    for mask in (first, jnp.logical_not(first)):
        q_one = jnp.where(mask, q, jnp.zeros_like(q))
        scores = lax.dot_general(
            q_one, k, (((1,), (1,)), ((), ())), preferred_element_type=jnp.float32
        ) * scale
        expo = jnp.exp(scores)
        total = jnp.sum(expo, axis=-1, keepdims=True)
        mixed = jnp.dot(expo.astype(jnp.bfloat16), v, preferred_element_type=jnp.float32)
        outs.append(mixed / total)
    o_ref[...] = jnp.where(first, outs[0], outs[1]).astype(o_ref.dtype)


def spatial_attention(query, keys, values, block_rows=288):
    rows, width = query.shape
    count = keys.shape[0]
    lanes = 2 * (D // H)
    grid = (width // lanes, rows // block_rows)
    return pl.pallas_call(
        pair_attention_kernel,
        out_shape=jax.ShapeDtypeStruct((rows, width), jnp.bfloat16),
        grid=grid,
        in_specs=[
            pl.BlockSpec((block_rows, lanes), lambda h, r: (r, h)),
            pl.BlockSpec((count, lanes), lambda h, r: (0, h)),
            pl.BlockSpec((count, lanes), lambda h, r: (0, h)),
        ],
        out_specs=pl.BlockSpec((block_rows, lanes), lambda h, r: (r, h)),
    )(query, keys, values)


def tempo(query, keys, values, valid):
    tokens, width = query.shape
    head_size = width // H
    scale = head_size ** (-0.5)
    q_heads = query.reshape(tokens, H, head_size)
    k_heads = keys.reshape(-1, tokens, H, head_size)
    v_heads = values.reshape(-1, tokens, H, head_size)
    scores = (
        jnp.einsum("nhd,wnhd->nhw", q_heads, k_heads, preferred_element_type=jnp.float32) * scale
    )
    expo = jnp.where(valid, jnp.exp(scores), 0.0)
    mixed = jnp.einsum(
        "nhw,wnhd->nhd", expo.astype(jnp.bfloat16), v_heads, preferred_element_type=jnp.float32
    )
    mixed = mixed / jnp.sum(expo, axis=-1)[..., None]
    return mixed.astype(jnp.bfloat16).reshape(tokens, width)


def local(
    patches,
    patch_weight,
    conv_taps,
    gain_space,
    qkv_space,
    out_space,
    gain_time,
    qkv_time,
    out_time,
):
    frames, zdev, grid, _, patch = patches.shape
    width = patch_weight.shape[1]
    tokens = zdev * grid * grid
    embed = jnp.dot(
        patches.reshape(-1, patch), patch_weight, preferred_element_type=jnp.float32
    ).astype(jnp.bfloat16)
    embed = embed.reshape(frames, zdev, grid, grid, width)
    padded = extended(embed, (("tok", 1),), 1)
    padded = jnp.pad(padded, ((0, 0), (0, 0), (1, 1), (1, 1), (0, 0)))
    conv = jnp.zeros((frames, zdev, grid, grid, width), jnp.float32)
    for dz in range(3):
        for dy in range(3):
            for dx in range(3):
                tap = conv_taps[9 * dz + 3 * dy + dx].astype(jnp.float32)
                conv = conv + tap * padded[
                    :, dz : dz + zdev, dy : dy + grid, dx : dx + grid
                ].astype(jnp.float32)
    stream = (embed.astype(jnp.float32) + conv).astype(jnp.bfloat16).reshape(frames, tokens, width)
    normed = rms_scale(stream.astype(jnp.float32), gain_space).astype(jnp.bfloat16)
    proj = jnp.dot(normed.reshape(-1, width), qkv_space, preferred_element_type=jnp.float32).astype(
        jnp.bfloat16
    )
    proj = proj.reshape(frames, tokens, 3 * width)
    query = proj[0, :, :width]
    own_kv = proj[0, :, width:]
    count = lax.axis_size("tok")
    other_kv = lax.ppermute(own_kv, "tok", [(i, (i + 1) % count) for i in range(count)])
    all_kv = jnp.concatenate([own_kv, other_kv], axis=0)
    spatial = spatial_attention(query, all_kv[:, :width], all_kv[:, width:])
    attn_proj = jnp.dot(
        spatial.reshape(-1, width), out_space, preferred_element_type=jnp.float32
    ).reshape(frames, tokens, width)
    stream2 = (stream.astype(jnp.float32) + attn_proj).astype(jnp.bfloat16)
    normed2 = rms_scale(stream2.astype(jnp.float32), gain_time).astype(jnp.bfloat16)
    proj2 = jnp.dot(
        normed2.reshape(-1, width), qkv_time, preferred_element_type=jnp.float32
    ).astype(jnp.bfloat16)
    proj2 = proj2.reshape(frames, tokens, 3 * width)
    query2 = proj2[:, :, :width]
    hops = (WIN + frames - 1) // frames
    history = [normed2]
    moving = normed2
    for hop in range(hops):
        moving = from_behind(moving, "tm", 1)
        history.insert(0, moving)
    joined_in = jnp.concatenate(history[:-1], axis=1)
    joined_kv = jnp.dot(
        joined_in.reshape(-1, width), qkv_time[:, width:], preferred_element_type=jnp.float32
    ).astype(jnp.bfloat16)
    joined_kv = joined_kv.reshape(-1, tokens, 2 * width)
    own_kv = proj2[:, :, width:]
    joined_kv = jnp.concatenate([joined_kv, own_kv], axis=0)
    joined = jnp.stack([joined_kv[:, :, :width], joined_kv[:, :, width:]])
    joined = joined.reshape(2, -1, tokens, width)
    first = lax.axis_index("tm") * frames
    offsets = jnp.arange(WIN + 1, dtype=jnp.int32)
    valid = first + 0 - WIN + offsets >= 0
    results = [tempo(query2[0], joined[0], joined[1], valid)]
    temporal = jnp.stack(results)
    time_proj = jnp.dot(
        temporal.reshape(-1, width), out_time, preferred_element_type=jnp.float32
    ).reshape(frames, tokens, width)
    output = (stream2.astype(jnp.float32) + time_proj).astype(jnp.bfloat16)
    return output.reshape(frames, zdev, grid, grid, width)


def solution(mesh):
    placed = (P("tm", "tok", None, None, None), P(), P(), P(), P(), P(), P(), P(), P())
    return jax.shard_map(
        local,
        mesh=mesh,
        in_specs=placed,
        out_specs=P("tm", "tok", None, None, None),
        check_vma=False,
    )
```

profile of v0, /device:TPU:24, one launch (start us, length us, event | category | flops | bytes accessed | tf_op | source)
XLA Modules:
  0.0 194.9 jit_solution(11458111569218868475)
XLA Ops:
  0.0 1.5 reshape.366
  1.5 2.6 %convolution_convert_fusion.3 = bf16[864,512]{1,0:T(8,128)(2,1)} fusion(bf16[864,512]{1,0:T(8,128)(2,1)S(1)} %reshape.366, bf16[512,512]{1,0:T(8,128)(2,1)} %param.10), kind=kOutput, calls=%fused_computation.63 | convolution fusion | flops 453427200 | bytes 2293760 | tf_op jit(solution)/shard_map/dot_general | solution.py:135
  4.1 1.3 reshape.367
  5.4 1.8 collective-permute-start
  7.2 1.3 collective-permute-start.1
  8.6 1.9 collective-permute-done.1
  10.5 2.1 %select_maximum_fusion = bf16[1,8,14,14,512]{4,3,2,1,0:T(8,128)(2,1)S(1)} fusion(bf16[1,1,12,12,512]{4,3,2,1,0:T(8,128)(2,1)S(1)} %collective-permute-done.1, bf16[1,6,12,12,512]{4,3,2,1,0:T(8,128)(2,1)} %copy-done.2, bf16[1,1,12,12,512]{4,3,2,1,0:T(8,128)(2,1)S(1)} %collective-permute-done), kind=kLoop, calls=%fused_computation.48 | loop fusion | flops 15253504 | bytes 2785280 | tf_op jit(solution)/shard_map/concatenate | solution.py:23
  12.6 10.2 %multiply_reduce_fusion.2 = (f32[6,12,12]{2,1,0:T(8,128)S(1)}, f32[1,6,12,12,512]{4,3,2,1,0:T(8,128)}) fusion(bf16[1,8,14,14,512]{4,3,2,1,0:T(8,128)(2,1)S(1)} %select_maximum_fusion, f32[512]{0:T(512)S(1)} %bitcast.87, f32[512]{0:T(512)S(1)} %bitcast.88, f32[512]{0:T(512)S(1)} %bitcast.63, f32[512]{0:T(512)S(1)} %bitcast.64, ...), kind=kLoop, calls=%fused_computation.46 | loop fusion | flops 38485152 | bytes 24241536 | tf_op jit(solution)/shard_map/reduce_sum | solution.py:34
  22.8 0.1 rsqrt.20
  22.9 1.7 reshape.400
  24.6 1.2 copy-done.5
  25.9 1.6 fusion.10
  27.5 0.2 slice_bitcast_fusion
  27.7 0.2 collective-permute-start.2
  28.0 0.2 copy-done.12
  28.2 1.0 slice_bitcast_fusion.1.q_ref
  29.1 2.4 %collective-permute-done.2 = bf16[864,1024]{1,0:T(8,128)(2,1)S(1)} collective-permute-done((bf16[864,1024]{1,0:T(8,128)(2,1)S(1)}, bf16[864,1024]{1,0:T(8,128)(2,1)S(1)}, u32[]{:S(2)}, u32[]{:S(2)}) %collective-permute-start.2) | collective-permute-done | bytes 1769504 | tf_op jit(solution)/shard_map/ppermute | solution.py:158
  31.5 2.1 %pad_maximum_fusion.1 = (bf16[1728,512]{1,0:T(8,128)(2,1)}, bf16[1728,512]{1,0:T(8,128)(2,1)}) fusion(bf16[864,1024]{1,0:T(8,128)(2,1)S(1)} %collective-permute-done.2, bf16[864,1024]{1,0:T(8,128)(2,1)S(1)} %slice_bitcast_fusion), kind=kLoop, calls=%fused_computation.59 | loop fusion | flops 7077888 | bytes 7077888 | tf_op jit(solution)/shard_map/concatenate | solution.py:159
  33.6 18.6 %shard_map.91 = bf16[864,512]{1,0:T(8,128)(2,1)} custom-call(bf16[864,512]{1,0:T(8,128)(2,1)} %slice_bitcast_fusion.1.q_ref, bf16[1728,512]{1,0:T(8,128)(2,1)} %get-tuple-element.10.k_ref, bf16[1728,512]{1,0:T(8,128)(2,1)} %get-tuple-element.9.v_ref), custom_call_target="tpu_custom_call" | custom-call | tf_op jit(solution)/shard_map/pallas_call | solution.py:90
  52.2 1.9 fusion.30
  54.1 0.3 fusion.39
  54.4 3.8 %collective-permute-start.3 = (bf16[1,864,512]{2,1,0:T(8,128)(2,1)S(1)}, bf16[1,864,512]{2,1,0:T(8,128)(2,1)S(1)}, u32[]{:S(2)}, u32[]{:S(2)}) collective-permute-start(bf16[1,864,512]{2,1,0:T(8,128)(2,1)S(1)} %fusion.39), channel_id=1, source_target_pairs={{0,2},{2,4},{4,6},{6,8},{8,10},{10,12},{12,14},{14,16},{16,18},{18... | collective-permute-start | bytes 2654216 | tf_op jit(solution)/shard_map/ppermute | solution.py:30
  58.2 26.2 %collective-permute-done.3 = bf16[1,864,512]{2,1,0:T(8,128)(2,1)S(1)} collective-permute-done((bf16[1,864,512]{2,1,0:T(8,128)(2,1)S(1)}, bf16[1,864,512]{2,1,0:T(8,128)(2,1)S(1)}, u32[]{:S(2)}, u32[]{:S(2)}) %collective-permute-start.3) | collective-permute-done | bytes 884768 | tf_op jit(solution)/shard_map/ppermute | solution.py:30
  84.4 1.9 collective-permute-start.4
  86.4 25.4 %collective-permute-done.4 = bf16[1,864,512]{2,1,0:T(8,128)(2,1)S(1)} collective-permute-done((bf16[1,864,512]{2,1,0:T(8,128)(2,1)S(1)}, bf16[1,864,512]{2,1,0:T(8,128)(2,1)S(1)}, u32[]{:S(2)}, u32[]{:S(2)}) %collective-permute-start.4) | collective-permute-done | bytes 884768 | tf_op jit(solution)/shard_map/ppermute | solution.py:30
  111.7 1.9 collective-permute-start.5
  113.7 24.6 %collective-permute-done.5 = bf16[1,864,512]{2,1,0:T(8,128)(2,1)} collective-permute-done((bf16[1,864,512]{2,1,0:T(8,128)(2,1)S(1)}, bf16[1,864,512]{2,1,0:T(8,128)(2,1)}, u32[]{:S(2)}, u32[]{:S(2)}) %collective-permute-start.5) | collective-permute-done | bytes 884768 | tf_op jit(solution)/shard_map/ppermute | solution.py:30
  138.2 2.1 %collective-permute-start.6 = (bf16[1,864,512]{2,1,0:T(8,128)(2,1)}, bf16[1,864,512]{2,1,0:T(8,128)(2,1)}, u32[]{:S(2)}, u32[]{:S(2)}) collective-permute-start(bf16[1,864,512]{2,1,0:T(8,128)(2,1)} %collective-permute-done.5), channel_id=1, source_target_pairs={{0,2},{2,4},{4,6},{6,8},{8,10},{10,12},{12,14},{14,16},{16,18},{18... | collective-permute-start | bytes 2654216 | tf_op jit(solution)/shard_map/ppermute | solution.py:30
  140.4 3.0 %fusion.11 = bf16[1,864,1536]{2,1,0:T(8,128)(2,1)S(1)} fusion(bf16[512,1536]{1,0:T(8,128)(2,1)} %param.16, bf16[864,512]{1,0:T(8,128)(2,1)S(1)} %get-tuple-element.43, f32[512]{0:T(512)S(1)} %convert_element_type.522, f32[864]{0:T(1024)S(1)} %add_rsqrt_fusion.1), kind=kOutput, calls=%fused_computation.26 | convolution fusion | flops 1362051072 | bytes 5117312 | tf_op jit(solution)/shard_map/dot_general | solution.py:166
  143.4 0.1 slice.292
  143.4 1.5 slice.293
  145.0 0.6 copy.13
  145.6 3.0 %copy.15 = bf16[1,864,1024]{1,2,0:T(8,128)(2,1)S(1)} copy(bf16[1,864,1024]{2,1,0:T(8,128)(2,1)} %slice.293) | data formatting | bytes 3538944 | tf_op jit(solution)/shard_map/slice | solution.py:182
  148.6 0.0 copy-start.13
  148.6 1.4 convert.28
  150.0 14.0 %collective-permute-done.6 = bf16[1,864,512]{2,1,0:T(8,128)(2,1)} collective-permute-done((bf16[1,864,512]{2,1,0:T(8,128)(2,1)}, bf16[1,864,512]{2,1,0:T(8,128)(2,1)}, u32[]{:S(2)}, u32[]{:S(2)}) %collective-permute-start.6) | collective-permute-done | bytes 884768 | tf_op jit(solution)/shard_map/ppermute | solution.py:30
  164.0 8.5 %convolution_convert_fusion = bf16[3456,1024]{1,0:T(8,128)(2,1)} fusion(bf16[1,864,512]{2,1,0:T(8,128)(2,1)S(1)} %copy-done.15, bf16[1,864,512]{2,1,0:T(8,128)(2,1)} %copy-done.16, bf16[1,864,512]{2,1,0:T(8,128)(2,1)} %collective-permute-done.5, bf16[1,864,512]{2,1,0:T(8,128)(2,1)} %collective-permute-done.6, bf16[512,1536]{1,0:T(8,128)(2,1)S(1)} %copy-done.13), kind=kOutput, calls=%fused_computation.4 | convolution fusion | flops 3641573376 | bytes 11665408 | tf_op jit(solution)/shard_map/dot_general | solution.py:178
  172.5 10.8 %copy.14 = bf16[4,864,1024]{1,2,0:T(8,128)(2,1)} copy(bf16[4,864,1024]{2,1,0:T(8,128)(2,1)} %bitcast.59) | data formatting | bytes 14155776 | tf_op jit(solution)/shard_map/reshape | solution.py:181
  183.3 4.0 %fusion = (bf16[5,864,512]{1,2,0:T(8,128)(2,1)S(1)}, bf16[5,864,512]{1,2,0:T(8,128)(2,1)S(1)}) fusion(bf16[4,864,1024]{1,2,0:T(8,128)(2,1)} %copy.14, bf16[1,864,1024]{1,2,0:T(8,128)(2,1)S(1)} %copy.15), kind=kLoop, calls=%fused_computation.9 | loop fusion | flops 17694720 | bytes 17694720 | tf_op jit(solution)/shard_map/concatenate | solution.py:183
  187.3 1.3 multiply_reduce_fusion.1
  188.6 0.1 fusion.41
  188.7 1.1 multiply_reduce_fusion
  189.8 0.0 copy-start.8
  189.9 0.2 divide_convert_fusion
  190.1 1.0 copy-done.8
  191.0 0.1 copy-done.17
  191.2 1.6 fusion.33
  192.7 2.1 %reshape.372 = bf16[1,6,12,12,512]{4,3,2,1,0:T(8,128)(2,1)} reshape(bf16[864,512]{1,0:T(8,128)(2,1)} %fusion.33) | data formatting | bytes 1769472 | tf_op jit(solution)/shard_map/reshape | solution.py:195
  (39 shorter events, 0.2 us)
Async XLA Ops:
  0.0 25.9 %copy-start = (bf16[512,1536]{1,0:T(8,128)(2,1)S(1)}, bf16[512,1536]{1,0:T(8,128)(2,1)}, u32[]{:S(2)}) copy-start(bf16[512,1536]{1,0:T(8,128)(2,1)} %param.13) | copy-start | bytes 4718596
  1.5 7.0 %copy-start.11 = (bf16[512]{0:T(512)(128)(2,1)S(1)}, bf16[512]{0:T(512)(128)(2,1)}, u32[]{:S(2)}) copy-start(bf16[512]{0:T(512)(128)(2,1)} %param.12) | copy-start | bytes 3076
  1.5 7.0 %copy-start.10 = (bf16[27,512]{1,0:T(8,128)(2,1)S(1)}, bf16[27,512]{1,0:T(8,128)(2,1)}, u32[]{:S(2)}) copy-start(bf16[27,512]{1,0:T(8,128)(2,1)} %param.11) | copy-start | bytes 82948
  5.4 3.2 %copy-start.2 = (bf16[1,6,12,12,512]{4,3,2,1,0:T(8,128)(2,1)}, bf16[1,6,12,12,512]{4,3,2,1,0:T(8,128)(2,1)S(1)}, u32[]{:S(2)}) copy-start(bf16[1,6,12,12,512]{4,3,2,1,0:T(8,128)(2,1)S(1)} %reshape.367) | copy-start | bytes 2654212
  5.4 3.2 %collective-permute-start = (bf16[1,1,12,12,512]{4,3,2,1,0:T(8,128)(2,1)S(1)}, bf16[1,1,12,12,512]{4,3,2,1,0:T(8,128)(2,1)S(1)}, u32[]{:S(2)}, u32[]{:S(2)}) collective-permute-start(bf16[1,1,12,12,512]{4,3,2,1,0:T(8,128)(2,1)S(1)} %get-tuple-element.11), channel_id=1, source_target_pairs={{0,1},{2,3},{4,5},{6,7},{8,9},{10,11},{12,13},{14,15},{16,17},{18,... | collective-permute-start | bytes 442376 | tf_op jit(solution)/shard_map/ppermute | solution.py:19
  7.2 3.3 %collective-permute-start.1 = (bf16[1,1,12,12,512]{4,3,2,1,0:T(8,128)(2,1)S(1)}, bf16[1,1,12,12,512]{4,3,2,1,0:T(8,128)(2,1)S(1)}, u32[]{:S(2)}, u32[]{:S(2)}) collective-permute-start(bf16[1,1,12,12,512]{4,3,2,1,0:T(8,128)(2,1)S(1)} %get-tuple-element.12), channel_id=1, source_target_pairs={{1,0},{3,2},{5,4},{7,6},{9,8},{11,10},{13,12},{15,14},{17,16},{19,... | collective-permute-start | bytes 442376 | tf_op jit(solution)/shard_map/ppermute | solution.py:22
  10.5 2.1 %copy-start.3 = (bf16[1,6,12,12,512]{4,3,2,1,0:T(8,128)(2,1)S(1)}, bf16[1,6,12,12,512]{4,3,2,1,0:T(8,128)(2,1)}, u32[]{:S(2)}) copy-start(bf16[1,6,12,12,512]{4,3,2,1,0:T(8,128)(2,1)} %copy-done.2) | copy-start | bytes 2654212
  24.6 1.3 copy-start.5
  27.5 0.7 copy-start.12
  27.7 3.8 %collective-permute-start.2 = (bf16[864,1024]{1,0:T(8,128)(2,1)S(1)}, bf16[864,1024]{1,0:T(8,128)(2,1)S(1)}, u32[]{:S(2)}, u32[]{:S(2)}) collective-permute-start(bf16[864,1024]{1,0:T(8,128)(2,1)S(1)} %slice_bitcast_fusion), channel_id=1, source_target_pairs={{0,1},{1,0},{2,3},{3,2},{4,5},{5,4},{6,7},{7,6},{8,9},{9,8},{10,11... | collective-permute-start | bytes 5308424 | tf_op jit(solution)/shard_map/ppermute | solution.py:158
  33.6 18.6 %copy-start.6 = (f32[864,512]{1,0:T(8,128)S(1)}, f32[864,512]{1,0:T(8,128)}, u32[]{:S(2)}) copy-start(f32[864,512]{1,0:T(8,128)} %copy-done.5) | copy-start | bytes 5308420
  33.6 18.6 %copy-start.9 = (bf16[512,512]{1,0:T(8,128)(2,1)S(1)}, bf16[512,512]{1,0:T(8,128)(2,1)}, u32[]{:S(2)}) copy-start(bf16[512,512]{1,0:T(8,128)(2,1)} %param.14) | copy-start | bytes 1572868
  54.1 89.3 %copy-start.7 = (bf16[864,512]{1,0:T(8,128)(2,1)}, bf16[864,512]{1,0:T(8,128)(2,1)S(1)}, u32[]{:S(2)}) copy-start(bf16[864,512]{1,0:T(8,128)(2,1)S(1)} %get-tuple-element.43) | copy-start | bytes 2654212
  54.4 30.1 %collective-permute-start.3 = (bf16[1,864,512]{2,1,0:T(8,128)(2,1)S(1)}, bf16[1,864,512]{2,1,0:T(8,128)(2,1)S(1)}, u32[]{:S(2)}, u32[]{:S(2)}) collective-permute-start(bf16[1,864,512]{2,1,0:T(8,128)(2,1)S(1)} %fusion.39), channel_id=1, source_target_pairs={{0,2},{2,4},{4,6},{6,8},{8,10},{10,12},{12,14},{14,16},{16,18},{18... | collective-permute-start | bytes 2654216 | tf_op jit(solution)/shard_map/ppermute | solution.py:30
  84.4 58.9 %copy-start.14 = (bf16[1,864,512]{2,1,0:T(8,128)(2,1)}, bf16[1,864,512]{2,1,0:T(8,128)(2,1)S(1)}, u32[]{:S(2)}) copy-start(bf16[1,864,512]{2,1,0:T(8,128)(2,1)S(1)} %collective-permute-done.3) | copy-start | bytes 2654212
  84.4 27.3 %collective-permute-start.4 = (bf16[1,864,512]{2,1,0:T(8,128)(2,1)S(1)}, bf16[1,864,512]{2,1,0:T(8,128)(2,1)S(1)}, u32[]{:S(2)}, u32[]{:S(2)}) collective-permute-start(bf16[1,864,512]{2,1,0:T(8,128)(2,1)S(1)} %collective-permute-done.3), channel_id=1, source_target_pairs={{0,2},{2,4},{4,6},{6,8},{8,10},{10,12},{12,14},{14,16},{16,18},{18... | collective-permute-start | bytes 2654216 | tf_op jit(solution)/shard_map/ppermute | solution.py:30
  111.7 28.6 %copy-start.16 = (bf16[1,864,512]{2,1,0:T(8,128)(2,1)}, bf16[1,864,512]{2,1,0:T(8,128)(2,1)S(1)}, u32[]{:S(2)}) copy-start(bf16[1,864,512]{2,1,0:T(8,128)(2,1)S(1)} %collective-permute-done.4) | copy-start | bytes 2654212
  111.7 26.5 %collective-permute-start.5 = (bf16[1,864,512]{2,1,0:T(8,128)(2,1)S(1)}, bf16[1,864,512]{2,1,0:T(8,128)(2,1)}, u32[]{:S(2)}, u32[]{:S(2)}) collective-permute-start(bf16[1,864,512]{2,1,0:T(8,128)(2,1)S(1)} %collective-permute-done.4), channel_id=1, source_target_pairs={{0,2},{2,4},{4,6},{6,8},{8,10},{10,12},{12,14},{14,16},{16,18},{18... | collective-permute-start | bytes 2654216 | tf_op jit(solution)/shard_map/ppermute | solution.py:30
  138.2 25.8 %collective-permute-start.6 = (bf16[1,864,512]{2,1,0:T(8,128)(2,1)}, bf16[1,864,512]{2,1,0:T(8,128)(2,1)}, u32[]{:S(2)}, u32[]{:S(2)}) collective-permute-start(bf16[1,864,512]{2,1,0:T(8,128)(2,1)} %collective-permute-done.5), channel_id=1, source_target_pairs={{0,2},{2,4},{4,6},{6,8},{8,10},{10,12},{12,14},{14,16},{16,18},{18... | collective-permute-start | bytes 2654216 | tf_op jit(solution)/shard_map/ppermute | solution.py:30
  148.6 15.4 %copy-start.13 = (bf16[512,1536]{1,0:T(8,128)(2,1)S(1)}, bf16[512,1536]{1,0:T(8,128)(2,1)}, u32[]{:S(2)}) copy-start(bf16[512,1536]{1,0:T(8,128)(2,1)} %param.16) | copy-start | bytes 4718596
  148.6 15.4 %copy-start.15 = (bf16[1,864,512]{2,1,0:T(8,128)(2,1)S(1)}, bf16[1,864,512]{2,1,0:T(8,128)(2,1)}, u32[]{:S(2)}) copy-start(bf16[1,864,512]{2,1,0:T(8,128)(2,1)} %copy-done.14) | copy-start | bytes 2654212
  183.3 4.0 %copy-start.4 = (f32[864,8,64]{0,2,1:T(8,128)S(1)}, f32[864,8,64]{0,2,1:T(8,128)}, u32[]{:S(2)}) copy-start(f32[864,8,64]{0,2,1:T(8,128)} %convert.28) | copy-start | bytes 5308420
  189.8 1.2 copy-start.8
  189.9 1.3 copy-start.17
  190.0 4.8 %copy-start.1 = (bf16[512,1536]{1,0:T(8,128)(2,1)S(1)}, bf16[512,1536]{1,0:T(8,128)(2,1)}, u32[]{:S(2)}) copy-start(bf16[512,1536]{1,0:T(8,128)(2,1)} %param.13) | copy-start | bytes 4718596
where the time goes:
time: 196 us; the launch traced here: 195 us
  waiting for transfers between devices  94.4 us (48%)
  local copies, waits for them, and re-layouts  26.6 us (14%)
  other arithmetic  22.7 us (12%)
  matrix products  19.1 us (10%)
  Pallas kernels  18.6 us (9%)
  starting transfers between devices  13 us (7%)
    ppermute x4, waiting for transfers between devices, from_behind(): lax.ppermute(value, axis, [(source, source + steps) for source in range(l...  90.2 us
    pallas_call x1, Pallas kernels, spatial_attention(): pl.pallas_call(pair_attention_kernel, out_shape=jax.ShapeDtypeStruct((row...  18.6 us
    reshape x1, local copies, waits for them, and re-layouts, local(): joined_kv = joined_kv.reshape(-1, tokens, 2 * width)  10.8 us
    reduce_sum x1, other arithmetic, rms_scale(): mean_sq = jnp.mean(values * values, axis=-1, keepdims=True)  10.2 us
    ppermute x4, starting transfers between devices, from_behind(): lax.ppermute(value, axis, [(source, source + steps) for source in range(l...  9.74 us
    dot_general x1, matrix products, local(): jnp.dot(joined_in.reshape(-1, width), qkv_time[:, width:], preferred_elem...  8.47 us
    slice x2, local copies, waits for them, and re-layouts, local(): own_kv = proj2[:, :, width:]  4.58 us
    concatenate x1, other arithmetic, local(): joined_kv = jnp.concatenate([joined_kv, own_kv], axis=0)  3.99 us
  transfers between devices with their start and end apart: 7, of which 6 were waited for; matrix products, arithmetic and copies ran while one was open for 5% of the time, Pallas kernels for 0%

commit v1 on v0

--- a/solution.py
+++ b/solution.py
@@ -100,24 +100,6 @@
     )(query, keys, values)
 
 
-def tempo(query, keys, values, valid):
-    tokens, width = query.shape
-    head_size = width // H
-    scale = head_size ** (-0.5)
-    q_heads = query.reshape(tokens, H, head_size)
-    k_heads = keys.reshape(-1, tokens, H, head_size)
-    v_heads = values.reshape(-1, tokens, H, head_size)
-    scores = (
-        jnp.einsum("nhd,wnhd->nhw", q_heads, k_heads, preferred_element_type=jnp.float32) * scale
-    )
-    expo = jnp.where(valid, jnp.exp(scores), 0.0)
-    mixed = jnp.einsum(
-        "nhw,wnhd->nhd", expo.astype(jnp.bfloat16), v_heads, preferred_element_type=jnp.float32
-    )
-    mixed = mixed / jnp.sum(expo, axis=-1)[..., None]
-    return mixed.astype(jnp.bfloat16).reshape(tokens, width)
-
-
 def local(
     patches,
     patch_weight,
@@ -167,27 +149,35 @@
         normed2.reshape(-1, width), qkv_time, preferred_element_type=jnp.float32
     ).astype(jnp.bfloat16)
     proj2 = proj2.reshape(frames, tokens, 3 * width)
-    query2 = proj2[:, :, :width]
-    hops = (WIN + frames - 1) // frames
-    history = [normed2]
-    moving = normed2
-    for hop in range(hops):
+    query2 = proj2[0, :, :width].astype(jnp.float32)
+    kv_weight = qkv_time[:, width:]
+    heads = lax.broadcasted_iota(jnp.int32, (width, width), 0) // (width // H)
+    same_head = heads == lax.broadcasted_iota(jnp.int32, (width, width), 1) // (width // H)
+    summer = jnp.concatenate([same_head, same_head], axis=0).astype(jnp.bfloat16)
+    scale = (width // H) ** (-0.5)
+
+    def time_term(kv, valid):
+        keys2 = kv[:, :width].astype(jnp.float32)
+        values2 = kv[:, width:].astype(jnp.float32)
+        prod = query2 * keys2
+        high = prod.astype(jnp.bfloat16)
+        low = (prod - high.astype(jnp.float32)).astype(jnp.bfloat16)
+        scores = jnp.dot(
+            jnp.concatenate([high, low], axis=1), summer, preferred_element_type=jnp.float32
+        ) * scale
+        expo = jnp.where(valid, jnp.exp(scores), 0.0)
+        return expo.astype(jnp.bfloat16).astype(jnp.float32) * values2, expo
+
+    first = lax.axis_index("tm") * frames
+    mixed, total = time_term(proj2[0, :, width:], True)
+    moving = normed2[0]
+    for back in range(1, WIN + 1):
         moving = from_behind(moving, "tm", 1)
-        history.insert(0, moving)
-    joined_in = jnp.concatenate(history[:-1], axis=1)
-    joined_kv = jnp.dot(
-        joined_in.reshape(-1, width), qkv_time[:, width:], preferred_element_type=jnp.float32
-    ).astype(jnp.bfloat16)
-    joined_kv = joined_kv.reshape(-1, tokens, 2 * width)
-    own_kv = proj2[:, :, width:]
-    joined_kv = jnp.concatenate([joined_kv, own_kv], axis=0)
-    joined = jnp.stack([joined_kv[:, :, :width], joined_kv[:, :, width:]])
-    joined = joined.reshape(2, -1, tokens, width)
-    first = lax.axis_index("tm") * frames
-    offsets = jnp.arange(WIN + 1, dtype=jnp.int32)
-    valid = first + 0 - WIN + offsets >= 0
-    results = [tempo(query2[0], joined[0], joined[1], valid)]
-    temporal = jnp.stack(results)
+        kv = jnp.dot(moving, kv_weight, preferred_element_type=jnp.float32).astype(jnp.bfloat16)
+        part, expo = time_term(kv, first - back >= 0)
+        mixed = mixed + part
+        total = total + expo
+    temporal = (mixed / total).astype(jnp.bfloat16)
     time_proj = jnp.dot(
         temporal.reshape(-1, width), out_time, preferred_element_type=jnp.float32
     ).reshape(frames, tokens, width)

time: 196 us -> 188 us (0.959)
  local copies, waits for them, and re-layouts: 26.6 us -> 8.44 us
  matrix products: 19.1 us -> 35.1 us
  other arithmetic: 22.7 us -> 17.3 us
    reshape x1 -> x0, local copies, waits for them, and re-layouts: 10.8 us -> none  [local(): joined_kv = joined_kv.reshape(-1, tokens, 2 * width)]
    dot_general x1, matrix products: 1.57 us -> 10.4 us  [local(): jnp.dot(temporal.reshape(-1, width), out_time, preferred_element_type=jnp...]
    dot_general x1 -> x8, matrix products: 8.47 us -> 15.6 us  [the longest x4 9.51 us: time_term(): jnp.dot(jnp.concatenate([high, low], axis=1), summer, preferred_element_t...]
    slice x4 -> x0, local copies, waits for them, and re-layouts: 5.22 us -> none  [the longest x2 4.58 us: local(): own_kv = proj2[:, :, width:]]
    concatenate x1 -> x0, other arithmetic: 3.99 us -> none  [local(): joined_kv = jnp.concatenate([joined_kv, own_kv], axis=0)]
    unnamed x36 -> x26, local copies, waits for them, and re-layouts: 2.66 us -> 0.24 us
    dot_general x2 -> x0, other arithmetic: 2.39 us -> none  [the longest x1 1.26 us: tempo(): jnp.einsum('nhd,wnhd->nhw', q_heads, k_heads, preferred_element_type=jnp....]
    convert_element_type x1, other arithmetic: 0.16 us -> 2.53 us  [time_term(): low = (prod - high.astype(jnp.float32)).astype(jnp.bfloat16)]
where the time goes in v1:
time: 188 us
  waiting for transfers between devices  95.4 us (51%)
  matrix products  35.1 us (19%)
  Pallas kernels  18.4 us (10%)
  other arithmetic  17.3 us (9%)
  starting transfers between devices  13 us (7%)
  local copies, waits for them, and re-layouts  8.44 us (4%)
    ppermute x4, waiting for transfers between devices, from_behind(): lax.ppermute(value, axis, [(source, source + steps) for source in range(l...  91 us
    pallas_call x1, Pallas kernels, spatial_attention(): pl.pallas_call(pair_attention_kernel, out_shape=jax.ShapeDtypeStruct((row...  18.4 us
    dot_general x1, matrix products, local(): jnp.dot(temporal.reshape(-1, width), out_time, preferred_element_type=jnp...  10.4 us
    reduce_sum x1, other arithmetic, rms_scale(): mean_sq = jnp.mean(values * values, axis=-1, keepdims=True)  10.1 us
    ppermute x4, starting transfers between devices, from_behind(): lax.ppermute(value, axis, [(source, source + steps) for source in range(l...  9.73 us
    dot_general x4, matrix products, time_term(): jnp.dot(jnp.concatenate([high, low], axis=1), summer, preferred_element_t...  9.51 us
    dot_general x4, matrix products, local(): jnp.dot(moving, kv_weight, preferred_element_type=jnp.float32)  6.13 us
  transfers between devices with their start and end apart: 7, of which 6 were waited for; matrix products, arithmetic and copies ran while one was open for 5% of the time, Pallas kernels for 0%

profile of v1, /device:TPU:24, one launch (start us, length us, event | category | flops | bytes accessed | tf_op | source)
XLA Modules:
  0.0 188.0 jit_solution(4016485325221392627)
XLA Ops:
  0.0 1.5 reshape.361
  1.5 0.0 copy-done.12
  1.5 1.5 convolution_convert_fusion.6
  3.1 1.3 reshape.362
  4.4 1.8 collective-permute-start
  6.1 1.3 collective-permute-start.1
  7.5 0.0 copy-done.7
  7.5 0.0 collective-permute-done
  7.5 1.9 %collective-permute-done.1 = bf16[1,1,12,12,512]{4,3,2,1,0:T(8,128)(2,1)S(1)} collective-permute-done((bf16[1,1,12,12,512]{4,3,2,1,0:T(8,128)(2,1)S(1)}, bf16[1,1,12,12,512]{4,3,2,1,0:T(8,128)(2,1)S(1)}, u32[]{:S(2)}, u32[]{:S(2)}) %collective-permute-start.1) | collective-permute-done | bytes 147488 | tf_op jit(solution)/shard_map/ppermute | solution.py:22
  9.5 0.9 select_maximum_fusion
  10.4 10.1 %multiply_reduce_fusion = (f32[6,12,12]{2,1,0:T(8,128)S(1)}, f32[1,6,12,12,512]{4,3,2,1,0:T(8,128)}) fusion(bf16[1,8,14,14,512]{4,3,2,1,0:T(8,128)(2,1)S(1)} %select_maximum_fusion, f32[512]{0:T(512)S(1)} %bitcast.102, f32[512]{0:T(512)S(1)} %bitcast.103, f32[512]{0:T(512)S(1)} %bitcast.78, f32[512]{0:T(512)S(1)} %bitcast.79, ...), kind=kLoop, calls=%fused_computation.37 | loop fusion | flops 38485152 | bytes 24241536 | tf_op jit(solution)/shard_map/reduce_sum | solution.py:34
  20.4 1.7 reshape.393
  22.2 0.1 rsqrt.20
  22.3 0.0 copy-done
  22.3 1.6 fusion.3
  23.9 0.0 copy-start.8
  23.9 0.3 slice_bitcast_fusion.1
  24.2 0.2 collective-permute-start.2
  24.4 0.2 copy-done.8
  24.6 1.0 slice_bitcast_fusion.3.q_ref
  25.6 2.4 %collective-permute-done.2 = bf16[864,1024]{1,0:T(8,128)(2,1)S(1)} collective-permute-done((bf16[864,1024]{1,0:T(8,128)(2,1)S(1)}, bf16[864,1024]{1,0:T(8,128)(2,1)S(1)}, u32[]{:S(2)}, u32[]{:S(2)}) %collective-permute-start.2) | collective-permute-done | bytes 1769504 | tf_op jit(solution)/shard_map/ppermute | solution.py:140
  28.0 2.0 %pad_maximum_fusion = (bf16[1728,512]{1,0:T(8,128)(2,1)}, bf16[1728,512]{1,0:T(8,128)(2,1)}) fusion(bf16[864,1024]{1,0:T(8,128)(2,1)S(1)} %collective-permute-done.2, bf16[864,1024]{1,0:T(8,128)(2,1)S(1)} %slice_bitcast_fusion.1), kind=kLoop, calls=%fused_computation.51 | loop fusion | flops 7077888 | bytes 7077888 | tf_op jit(solution)/shard_map/concatenate | solution.py:141
  30.0 18.4 %shard_map.91 = bf16[864,512]{1,0:T(8,128)(2,1)} custom-call(bf16[864,512]{1,0:T(8,128)(2,1)} %slice_bitcast_fusion.3.q_ref, bf16[1728,512]{1,0:T(8,128)(2,1)} %get-tuple-element.18.k_ref, bf16[1728,512]{1,0:T(8,128)(2,1)} %get-tuple-element.17.v_ref), custom_call_target="tpu_custom_call" | custom-call | tf_op jit(solution)/shard_map/pallas_call | solution.py:90
  48.4 2.8 %fusion.23 = (f32[864]{0:T(1024)S(1)}, bf16[864,512]{1,0:T(8,128)(2,1)}) fusion(f32[864,512]{1,0:T(8,128)S(1)} %reshape.393, bf16[864,512]{1,0:T(8,128)(2,1)} %shard_map.91, bf16[512,512]{1,0:T(8,128)(2,1)} %param.14), kind=kOutput, calls=%fused_computation.45 | convolution fusion | flops 455195808 | bytes 4066688 | tf_op jit(solution)/shard_map/dot_general | solution.py:143
  51.3 1.4 fusion.25
  52.7 3.8 %collective-permute-start.3 = (bf16[864,512]{1,0:T(8,128)(2,1)S(1)}, bf16[864,512]{1,0:T(8,128)(2,1)S(1)}, u32[]{:S(2)}, u32[]{:S(2)}) collective-permute-start(bf16[864,512]{1,0:T(8,128)(2,1)S(1)} %fusion.25), channel_id=1, source_target_pairs={{0,2},{2,4},{4,6},{6,8},{8,10},{10,12},{12,14},{14,16},{16,18},{18... | collective-permute-start | bytes 2654216 | tf_op jit(solution)/shard_map/ppermute | solution.py:30
  56.5 26.3 %collective-permute-done.3 = bf16[864,512]{1,0:T(8,128)(2,1)S(1)} collective-permute-done((bf16[864,512]{1,0:T(8,128)(2,1)S(1)}, bf16[864,512]{1,0:T(8,128)(2,1)S(1)}, u32[]{:S(2)}, u32[]{:S(2)}) %collective-permute-start.3) | collective-permute-done | bytes 884768 | tf_op jit(solution)/shard_map/ppermute | solution.py:30
  82.8 1.9 %collective-permute-start.4 = (bf16[864,512]{1,0:T(8,128)(2,1)S(1)}, bf16[864,512]{1,0:T(8,128)(2,1)}, u32[]{:S(2)}, u32[]{:S(2)}) collective-permute-start(bf16[864,512]{1,0:T(8,128)(2,1)S(1)} %collective-permute-done.3), channel_id=1, source_target_pairs={{0,2},{2,4},{4,6},{6,8},{8,10},{10,12},{12,14},{14,16},{16,18},{18... | collective-permute-start | bytes 2654216 | tf_op jit(solution)/shard_map/ppermute | solution.py:30
  84.7 25.4 %collective-permute-done.4 = bf16[864,512]{1,0:T(8,128)(2,1)} collective-permute-done((bf16[864,512]{1,0:T(8,128)(2,1)S(1)}, bf16[864,512]{1,0:T(8,128)(2,1)}, u32[]{:S(2)}, u32[]{:S(2)}) %collective-permute-start.4) | collective-permute-done | bytes 884768 | tf_op jit(solution)/shard_map/ppermute | solution.py:30
  110.2 1.9 %collective-permute-start.5 = (bf16[864,512]{1,0:T(8,128)(2,1)}, bf16[864,512]{1,0:T(8,128)(2,1)S(1)}, u32[]{:S(2)}, u32[]{:S(2)}) collective-permute-start(bf16[864,512]{1,0:T(8,128)(2,1)} %collective-permute-done.4), channel_id=1, source_target_pairs={{0,2},{2,4},{4,6},{6,8},{8,10},{10,12},{12,14},{14,16},{16,18},{18... | collective-permute-start | bytes 2654216 | tf_op jit(solution)/shard_map/ppermute | solution.py:30
  112.1 0.3 select_compare_fusion
  112.4 3.0 %fusion.4 = bf16[1,864,1536]{2,1,0:T(8,128)(2,1)S(1)} fusion(bf16[864,512]{1,0:T(8,128)(2,1)S(1)} %fusion.25, bf16[512,1536]{1,0:T(8,128)(2,1)} %param.16), kind=kOutput, calls=%fused_computation.17 | convolution fusion | flops 1360281600 | bytes 5111808 | tf_op jit(solution)/shard_map/dot_general | solution.py:148
  115.4 0.0 copy-start.9
  115.5 0.2 slice_bitcast_fusion
  115.7 21.1 %collective-permute-done.5 = bf16[864,512]{1,0:T(8,128)(2,1)S(1)} collective-permute-done((bf16[864,512]{1,0:T(8,128)(2,1)}, bf16[864,512]{1,0:T(8,128)(2,1)S(1)}, u32[]{:S(2)}, u32[]{:S(2)}) %collective-permute-start.5) | collective-permute-done | bytes 884768 | tf_op jit(solution)/shard_map/ppermute | solution.py:30
  136.8 2.1 %collective-permute-start.6 = (bf16[864,512]{1,0:T(8,128)(2,1)S(1)}, bf16[864,512]{1,0:T(8,128)(2,1)S(1)}, u32[]{:S(2)}, u32[]{:S(2)}) collective-permute-start(bf16[864,512]{1,0:T(8,128)(2,1)S(1)} %collective-permute-done.5), channel_id=1, source_target_pairs={{0,2},{2,4},{4,6},{6,8},{8,10},{10,12},{12,14},{14,16},{16,18},{18... | collective-permute-start | bytes 2654216 | tf_op jit(solution)/shard_map/ppermute | solution.py:30
  138.9 1.1 convolution_convert_fusion.5
  140.0 2.9 %convolution_convert_fusion.4 = bf16[864,1024]{1,0:T(8,128)(2,1)S(1)} fusion(bf16[864,512]{1,0:T(8,128)(2,1)} %collective-permute-done.4, bf16[512,1536]{1,0:T(8,128)(2,1)S(1)} %copy-done.9), kind=kOutput, calls=%fused_computation.88 | convolution fusion | flops 906854400 | bytes 3702784 | tf_op jit(solution)/shard_map/dot_general | solution.py:176
  142.9 1.1 convolution_convert_fusion.3
  144.0 18.3 %collective-permute-done.6 = bf16[864,512]{1,0:T(8,128)(2,1)S(1)} collective-permute-done((bf16[864,512]{1,0:T(8,128)(2,1)S(1)}, bf16[864,512]{1,0:T(8,128)(2,1)S(1)}, u32[]{:S(2)}, u32[]{:S(2)}) %collective-permute-start.6) | collective-permute-done | bytes 884768 | tf_op jit(solution)/shard_map/ppermute | solution.py:30
  162.2 1.1 convolution_convert_fusion.2
  163.4 2.5 %subtract_convert_fusion = (bf16[864,512]{1,0:T(8,128)(2,1)}, bf16[864,512]{1,0:T(8,128)(2,1)}, bf16[864,512]{1,0:T(8,128)(2,1)S(1)}, bf16[864,512]{1,0:T(8,128)...) fusion(bf16[864,1024]{1,0:T(8,128)(2,1)S(1)} %convolution_conve, ...), kind=kLoop, calls=%fused_computation.75 | loop fusion | flops 13713408 | bytes 14155776 | tf_op jit(solution)/shard_map/convert_element_type | solution.py:164
  165.9 2.4 %fusion.28 = f32[864,512]{1,0:T(8,128)} fusion(bf16[864,512]{1,0:T(8,128)(2,1)S(1)} %get-tuple-element.25, bf16[864,512]{1,0:T(8,128)(2,1)S(1)} %get-tuple-element.26, pred[512,512]{1,0:T(32,128)(4,1)S(1)} %select_compare_fusion), kind=kOutput, calls=%fused_computation.53 | convolution fusion | flops 910032896 | bytes 3801088 | tf_op jit(solution)/shard_map/dot_general | solution.py:165
  168.3 2.4 %exponential_select_fusion.3 = f32[864,512]{1,0:T(8,128)} fusion(bf16[864,512]{1,0:T(8,128)(2,1)S(1)} %get-tuple-element.19, bf16[864,512]{1,0:T(8,128)(2,1)S(1)} %get-tuple-element.20, pred[]{:T(512)S(6)} %ge.12, pred[512,512]{1,0:T(32,128)(4,1)S(1)} %select_compare_fusion), kind=kOutput, calls=%fused_computation.80 | convolution fusion | flops 910917632 | bytes 3801089 | tf_op jit(solution)/shard_map/dot_general | solution.py:165
  170.7 2.4 %exponential_select_fusion.2 = f32[864,512]{1,0:T(8,128)} fusion(bf16[864,512]{1,0:T(8,128)(2,1)S(1)} %get-tuple-element.21, bf16[864,512]{1,0:T(8,128)(2,1)S(1)} %get-tuple-element.22, pred[]{:T(512)S(6)} %ge.13, pred[512,512]{1,0:T(32,128)(4,1)S(1)} %select_compare_fusion), kind=kOutput, calls=%fused_computation.78 | convolution fusion | flops 910917632 | bytes 3801089 | tf_op jit(solution)/shard_map/dot_general | solution.py:165
  173.1 2.4 %exponential_select_fusion.1 = f32[864,512]{1,0:T(8,128)} fusion(bf16[864,512]{1,0:T(8,128)(2,1)S(1)} %get-tuple-element.23, bf16[864,512]{1,0:T(8,128)(2,1)S(1)} %get-tuple-element.24, pred[]{:T(512)S(6)} %ge.14, pred[512,512]{1,0:T(32,128)(4,1)S(1)} %select_compare_fusion), kind=kOutput, calls=%fused_computation.76 | convolution fusion | flops 910917632 | bytes 3801089 | tf_op jit(solution)/shard_map/dot_general | solution.py:165
  175.4 10.4 %fusion.26 = bf16[864,512]{1,0:T(8,128)(2,1)} fusion(bf16[864,512]{1,0:T(8,128)(2,1)} %get-tuple-element.57, bf16[512,512]{1,0:T(8,128)(2,1)} %param.17, f32[864,512]{1,0:T(8,128)} %exponential_select_fusion.1, f32[864,512]{1,0:T(8,128)} %exponential_select_fusion.2, f32[864,512]{1,0:T(8,128)} %exponential_select_fusion.3, f32[864,512]{1,0:T(8,128)} %fusion.28, ...), kind=kOutput, calls=%fused_computation.48 | convolution fusion | flops 1378942976 | bytes 15826945 | tf_op jit(solution)/shard_map/dot_general | solution.py:181
  185.8 2.1 %reshape.365 = bf16[1,6,12,12,512]{4,3,2,1,0:T(8,128)(2,1)} reshape(bf16[864,512]{1,0:T(8,128)(2,1)} %fusion.26) | data formatting | bytes 1769472 | tf_op jit(solution)/shard_map/reshape | solution.py:185
  (29 shorter events, 0.2 us)
Async XLA Ops:
  0.0 22.3 %copy-start = (bf16[512,1536]{1,0:T(8,128)(2,1)S(1)}, bf16[512,1536]{1,0:T(8,128)(2,1)}, u32[]{:S(2)}) copy-start(bf16[512,1536]{1,0:T(8,128)(2,1)} %param.13) | copy-start | bytes 4718596
  0.0 1.5 copy-start.12
  3.1 4.4 %copy-start.6 = (bf16[27,512]{1,0:T(8,128)(2,1)S(1)}, bf16[27,512]{1,0:T(8,128)(2,1)}, u32[]{:S(2)}) copy-start(bf16[27,512]{1,0:T(8,128)(2,1)} %param.11) | copy-start | bytes 82948
  3.1 4.4 %copy-start.7 = (bf16[512]{0:T(512)(128)(2,1)S(1)}, bf16[512]{0:T(512)(128)(2,1)}, u32[]{:S(2)}) copy-start(bf16[512]{0:T(512)(128)(2,1)} %param.12) | copy-start | bytes 3076
  4.4 3.2 %collective-permute-start = (bf16[1,1,12,12,512]{4,3,2,1,0:T(8,128)(2,1)S(1)}, bf16[1,1,12,12,512]{4,3,2,1,0:T(8,128)(2,1)S(1)}, u32[]{:S(2)}, u32[]{:S(2)}) collective-permute-start(bf16[1,1,12,12,512]{4,3,2,1,0:T(8,128)(2,1)S(1)} %get-tuple-element.27), channel_id=1, source_target_pairs={{0,1},{2,3},{4,5},{6,7},{8,9},{10,11},{12,13},{14,15},{16,17},{18,... | collective-permute-start | bytes 442376 | tf_op jit(solution)/shard_map/ppermute | solution.py:19
  6.1 3.3 %collective-permute-start.1 = (bf16[1,1,12,12,512]{4,3,2,1,0:T(8,128)(2,1)S(1)}, bf16[1,1,12,12,512]{4,3,2,1,0:T(8,128)(2,1)S(1)}, u32[]{:S(2)}, u32[]{:S(2)}) collective-permute-start(bf16[1,1,12,12,512]{4,3,2,1,0:T(8,128)(2,1)S(1)} %get-tuple-element.28), channel_id=1, source_target_pairs={{1,0},{3,2},{5,4},{7,6},{9,8},{11,10},{13,12},{15,14},{17,16},{19,... | collective-permute-start | bytes 442376 | tf_op jit(solution)/shard_map/ppermute | solution.py:22
  23.9 0.7 copy-start.8
  24.2 3.8 %collective-permute-start.2 = (bf16[864,1024]{1,0:T(8,128)(2,1)S(1)}, bf16[864,1024]{1,0:T(8,128)(2,1)S(1)}, u32[]{:S(2)}, u32[]{:S(2)}) collective-permute-start(bf16[864,1024]{1,0:T(8,128)(2,1)S(1)} %slice_bitcast_fusion.1), channel_id=1, source_target_pairs={{0,1},{1,0},{2,3},{3,2},{4,5},{5,4},{6,7},{7,6},{8,9},{9,8},{10,11... | collective-permute-start | bytes 5308424 | tf_op jit(solution)/shard_map/ppermute | solution.py:140
  52.7 30.1 %collective-permute-start.3 = (bf16[864,512]{1,0:T(8,128)(2,1)S(1)}, bf16[864,512]{1,0:T(8,128)(2,1)S(1)}, u32[]{:S(2)}, u32[]{:S(2)}) collective-permute-start(bf16[864,512]{1,0:T(8,128)(2,1)S(1)} %fusion.25), channel_id=1, source_target_pairs={{0,2},{2,4},{4,6},{6,8},{8,10},{10,12},{12,14},{14,16},{16,18},{18... | collective-permute-start | bytes 2654216 | tf_op jit(solution)/shard_map/ppermute | solution.py:30
  82.8 29.6 %copy-start.10 = (bf16[864,512]{1,0:T(8,128)(2,1)}, bf16[864,512]{1,0:T(8,128)(2,1)S(1)}, u32[]{:S(2)}) copy-start(bf16[864,512]{1,0:T(8,128)(2,1)S(1)} %collective-permute-done.3) | copy-start | bytes 2654212
  82.8 27.4 %collective-permute-start.4 = (bf16[864,512]{1,0:T(8,128)(2,1)S(1)}, bf16[864,512]{1,0:T(8,128)(2,1)}, u32[]{:S(2)}, u32[]{:S(2)}) collective-permute-start(bf16[864,512]{1,0:T(8,128)(2,1)S(1)} %collective-permute-done.3), channel_id=1, source_target_pairs={{0,2},{2,4},{4,6},{6,8},{8,10},{10,12},{12,14},{14,16},{16,18},{18... | collective-permute-start | bytes 2654216 | tf_op jit(solution)/shard_map/ppermute | solution.py:30
  110.2 26.6 %collective-permute-start.5 = (bf16[864,512]{1,0:T(8,128)(2,1)}, bf16[864,512]{1,0:T(8,128)(2,1)S(1)}, u32[]{:S(2)}, u32[]{:S(2)}) collective-permute-start(bf16[864,512]{1,0:T(8,128)(2,1)} %collective-permute-done.4), channel_id=1, source_target_pairs={{0,2},{2,4},{4,6},{6,8},{8,10},{10,12},{12,14},{14,16},{16,18},{18... | collective-permute-start | bytes 2654216 | tf_op jit(solution)/shard_map/ppermute | solution.py:30
  112.4 60.7 %copy-start.5 = (pred[512,512]{1,0:T(32,128)(4,1)}, pred[512,512]{1,0:T(32,128)(4,1)S(1)}, u32[]{:S(2)}) copy-start(pred[512,512]{1,0:T(32,128)(4,1)S(1)} %select_compare_fusion) | copy-start | bytes 786436
  115.4 23.4 %copy-start.9 = (bf16[512,1536]{1,0:T(8,128)(2,1)S(1)}, bf16[512,1536]{1,0:T(8,128)(2,1)}, u32[]{:S(2)}) copy-start(bf16[512,1536]{1,0:T(8,128)(2,1)} %param.16) | copy-start | bytes 4718596
  115.4 23.4 %copy-start.11 = (bf16[864,512]{1,0:T(8,128)(2,1)S(1)}, bf16[864,512]{1,0:T(8,128)(2,1)}, u32[]{:S(2)}) copy-start(bf16[864,512]{1,0:T(8,128)(2,1)} %copy-done.10) | copy-start | bytes 2654212
  136.8 25.5 %collective-permute-start.6 = (bf16[864,512]{1,0:T(8,128)(2,1)S(1)}, bf16[864,512]{1,0:T(8,128)(2,1)S(1)}, u32[]{:S(2)}, u32[]{:S(2)}) collective-permute-start(bf16[864,512]{1,0:T(8,128)(2,1)S(1)} %collective-permute-done.5), channel_id=1, source_target_pairs={{0,2},{2,4},{4,6},{6,8},{8,10},{10,12},{12,14},{14,16},{16,18},{18... | collective-permute-start | bytes 2654216 | tf_op jit(solution)/shard_map/ppermute | solution.py:30
  140.0 23.4 %copy-start.1 = (bf16[864,1024]{1,0:T(8,128)(2,1)}, bf16[864,1024]{1,0:T(8,128)(2,1)S(1)}, u32[]{:S(2)}) copy-start(bf16[864,1024]{1,0:T(8,128)(2,1)S(1)} %convolution_convert_fusion.5) | copy-start | bytes 5308420
  142.9 20.5 %copy-start.2 = (bf16[864,1024]{1,0:T(8,128)(2,1)}, bf16[864,1024]{1,0:T(8,128)(2,1)S(1)}, u32[]{:S(2)}) copy-start(bf16[864,1024]{1,0:T(8,128)(2,1)S(1)} %convolution_convert_fusion.4) | copy-start | bytes 5308420
  144.0 19.4 %copy-start.3 = (bf16[864,1024]{1,0:T(8,128)(2,1)}, bf16[864,1024]{1,0:T(8,128)(2,1)S(1)}, u32[]{:S(2)}) copy-start(bf16[864,1024]{1,0:T(8,128)(2,1)S(1)} %convolution_convert_fusion.3) | copy-start | bytes 5308420
  163.4 2.5 %copy-start.4 = (bf16[864,1024]{1,0:T(8,128)(2,1)}, bf16[864,1024]{1,0:T(8,128)(2,1)S(1)}, u32[]{:S(2)}) copy-start(bf16[864,1024]{1,0:T(8,128)(2,1)S(1)} %convolution_convert_fusion.2) | copy-start | bytes 5308420
